TPU v7x, 32 devices: a whole 2x2x4 slice. The times are simulated.
32 devices in a mesh: wide: 8 (over z, y), narrow: 4 (over x, core).
Axes of the slice: x: 2, y: 2, z: 4, core: 2. Of those that a mesh axis runs over, the one named last changes fastest.
Arguments:
- spectra: bfloat16 [128, 32, 1024], P(None, 'narrow', 'wide'), may hold values from -6 to 6
- response: bfloat16 [12, 128, 32, 1024], P(None, None, 'narrow', 'wide'), may hold values from -0.5 to 0.5
- observed: bfloat16 [128, 32, 1024], P('wide', 'narrow'), may hold values from -6 to 6
- column_profile: float32 [32, 1024], P('wide'), as said below
- row_kernel: float32 [32, 5], P('wide'), may hold values from 0.1 to 0.4
- noise_weight: float32 [128], P('wide'), may hold values from 0.3 to 3
- cutoff: int32 [32], P('wide'), may hold values from 128 to 512
- owner: int32 [8], replicated, may hold values from 0 to 7, each once
Outputs:
- gradient: float32 [12, 32, 1024], P(None, 'narrow', 'wide')
Inputs may be any that keep to these rules, and one draw needn't show every extreme that they name: `owner`: each value 0 .. 7 appears once. `column_profile`: positive.
All inputs are finite; a program needn't handle non-finite values.
Results may differ from a plain program's by a relative error of at most 0.0029.
Values may be sent and summed in bfloat16 or wider, within the bound.
A program may use at most 64 MiB of HBM per device.

v0:
```python
import functools
import math

import jax
import jax.numpy as jnp
import numpy as np
from jax import lax
from jax.experimental import pallas as pl
from jax.experimental.pallas import tpu as pltpu
from jax.sharding import PartitionSpec as P


def with_halo(shard, sides, width):
    for axis, dim in sides:
        peers, length = (lax.axis_size(axis), shard.shape[dim])
        up = [(i, (i + 1) % peers) for i in range(peers - 1)]
        down = [(j, i) for i, j in up]
        last = lax.slice_in_dim(shard, length - width, length, axis=dim)
        leading = lax.slice_in_dim(shard, 0, width, axis=dim)
        before = lax.ppermute(last, axis, up)
        after = lax.ppermute(leading, axis, down)
        shard = jnp.concatenate([before, shard, after], axis=dim)
    return shard


def tile_order(values, owner, forward):
    count = owner.shape[0]
    tiles = jnp.arange(count, dtype=jnp.int32)
    select = (owner[None, :] == tiles[:, None]).astype(values.dtype)
    if forward:
        mixed = jnp.einsum("wsrak,at->wsrtk", values, select, preferred_element_type=jnp.float32)
    else:
        mixed = jnp.einsum("wsrtk,at->wsrak", values, select, preferred_element_type=jnp.float32)
    return mixed.astype(values.dtype)


def phase_table(size_in, size_out, period):
    left_index = jnp.arange(size_in, dtype=jnp.int32)[:, None]
    right_index = jnp.arange(size_out, dtype=jnp.int32)[None, :]
    angle = 2.0 * math.pi / period * (left_index * right_index % period).astype(jnp.float32)
    return (jnp.cos(angle), jnp.sin(angle))


def complex_product(form, value_real, value_imag, table_real, table_imag):

    def contract(left_side, right_side):
        return jnp.einsum(form, left_side, right_side, precision=lax.Precision.HIGHEST)

    if value_imag is None:
        return (contract(value_real, table_real), contract(value_real, table_imag))
    first_real = contract(value_real, table_real) - contract(value_imag, table_imag)
    first_imag = contract(value_real, table_imag) + contract(value_imag, table_real)
    return (first_real, first_imag)


def forward_transform(values, count, tile):
    columns = count * tile
    outer_cos, outer_sin = phase_table(count, count, count)
    segment_real, segment_imag = complex_product(
        "...tk,tf->...fk", values, None, outer_cos, -outer_sin
    )
    twist_cos, twist_sin = phase_table(count, tile, columns)
    turned_real = segment_real * twist_cos + segment_imag * twist_sin
    turned_imag = segment_imag * twist_cos - segment_real * twist_sin
    inner_cos, inner_sin = phase_table(tile, tile, tile)
    return complex_product("...fk,kg->...fg", turned_real, turned_imag, inner_cos, -inner_sin)


def inverse_transform(spec_real, spec_imag, count, tile):
    columns = count * tile
    inner_cos, inner_sin = phase_table(tile, tile, tile)
    segment_real, segment_imag = complex_product(
        "...fg,gk->...fk", spec_real, spec_imag, inner_cos, inner_sin
    )
    twist_cos, twist_sin = phase_table(count, tile, columns)
    turned_real = segment_real * twist_cos - segment_imag * twist_sin
    turned_imag = segment_imag * twist_cos + segment_real * twist_sin
    outer_cos, outer_sin = phase_table(count, count, count)
    real_part = jnp.einsum(
        "...fk,ft->...tk", turned_real, outer_cos, precision=lax.Precision.HIGHEST
    )
    real_part = real_part - jnp.einsum(
        "...fk,ft->...tk", turned_imag, outer_sin, precision=lax.Precision.HIGHEST
    )
    return real_part / columns


def band_transfer(column_profile, cutoff, count, tile):
    waves = column_profile.shape[0]
    columns = count * tile
    shaped = column_profile.reshape(waves, count, tile)
    gain_real, gain_imag = forward_transform(shaped, count, tile)
    low_index = jnp.arange(count, dtype=jnp.int32)[:, None]
    high_index = jnp.arange(tile, dtype=jnp.int32)[None, :]
    frequency = low_index + count * high_index
    distance = jnp.minimum(frequency, columns - frequency)
    keep = (distance[None, :, :] < cutoff[:, None, None]).astype(jnp.float32)
    return (gain_real * keep, gain_imag * keep)


def convolve(values, gain_real, gain_imag, adjoint):
    count, tile = (values.shape[-2], values.shape[-1])
    part_real, part_imag = forward_transform(values, count, tile)
    use_real = gain_real[:, None, None]
    use_imag = gain_imag[:, None, None]
    if adjoint:
        use_imag = -use_imag
    product_real = part_real * use_real - part_imag * use_imag
    product_imag = part_real * use_imag + part_imag * use_real
    return inverse_transform(product_real, product_imag, count, tile)


def row_blur(padded, kernel, extent, start_of):
    result = jnp.zeros(padded.shape[:2] + (extent, padded.shape[3]), jnp.float32)
    for lag in range(kernel.shape[1]):
        begin = start_of(lag)
        section = padded[:, :, begin : begin + extent].astype(jnp.float32)
        result = result + kernel[:, lag][:, None, None, None] * section
    return result


def strip_plan(
    spectra, response, observed, column_profile, row_kernel, noise_weight, cutoff, owner
):
    channels, rows, width = spectra.shape
    waves = column_profile.shape[0]
    columns = column_profile.shape[1]
    count = owner.shape[0]
    tile = columns // count
    half = (row_kernel.shape[1] - 1) // 2
    gain_real, gain_imag = band_transfer(column_profile, cutoff, count, tile)
    segmented = spectra.reshape(channels // 4, 4, rows, width)

    def forward(items):
        stokes = items.shape[1]
        tiled = items.reshape(waves, stokes, rows, count, tile)
        ordered = tile_order(tiled, owner, True)
        result = convolve(ordered.astype(jnp.float32), gain_real, gain_imag, False)
        return result.reshape(waves, stokes, rows, columns).astype(jnp.bfloat16)

    image = forward(lax.all_to_all(segmented, "wide", split_axis=0, concat_axis=3, tiled=True))
    target = observed.reshape(waves, 4, rows, columns)
    weights = noise_weight.reshape(waves, 4)[:, :, None, None]
    joined = with_halo(jnp.stack([image, target]), (("narrow", 3),), 2 * half)
    extent = rows + 2 * half
    blurred = row_blur(joined[0], row_kernel, extent, lambda lag: lag)
    observed_rows = joined[1, :, :, half : half + extent].astype(jnp.float32)
    global_rows = lax.axis_index("narrow") * rows - half + jnp.arange(extent, dtype=jnp.int32)
    inside = ((global_rows >= 0) & (global_rows < rows * lax.axis_size("narrow"))).astype(
        jnp.float32
    )
    padded_misfit = (weights * (blurred - observed_rows) * inside[:, None]).astype(jnp.bfloat16)
    spread = row_blur(padded_misfit, row_kernel, rows, lambda lag: 2 * half - lag)
    spread = spread.astype(jnp.bfloat16).reshape(waves, 4, rows, count, tile)
    back = convolve(spread.astype(jnp.float32), gain_real, gain_imag, True).astype(jnp.bfloat16)
    restored = tile_order(back, owner, False).reshape(waves, 4, rows, columns)
    returned = lax.all_to_all(restored, "wide", split_axis=3, concat_axis=0, tiled=True)
    pixels = returned.reshape(channels, rows, width)
    return jnp.einsum("pcrx,crx->prx", response, pixels, preferred_element_type=jnp.float32)


HALVES = 1
MESH = pl.DeviceIdType.MESH
HIGHEST = lax.Precision.HIGHEST


def phase_constants(count, tile):
    columns = count * tile
    inner = 2.0 * np.pi / tile * (np.outer(np.arange(tile), np.arange(tile)) % tile)
    wheel = np.concatenate([np.cos(inner), np.sin(inner)], axis=1)
    low = np.arange(count)[None, :, None]
    place = (np.arange(count)[:, None] * tile + np.arange(tile)[None, :])[:, None, :]
    turn = 2.0 * np.pi / columns * (low * place % columns)
    return (
        wheel.astype(np.float32),
        np.cos(turn).astype(np.float32),
        np.sin(turn).astype(np.float32),
    )


def band_kernel(profile, cut, wheel, turn_cos, turn_sin, count, tile):
    columns = count * tile
    real = jnp.zeros((count, tile), jnp.float32)
    imag = jnp.zeros((count, tile), jnp.float32)
    for t in range(count):
        piece = profile[:, t * tile : (t + 1) * tile]
        real = real + piece * turn_cos[t]
        imag = imag - piece * turn_sin[t]
    mixed = jnp.dot(
        jnp.concatenate([real, imag], axis=0),
        wheel,
        precision=HIGHEST,
        preferred_element_type=jnp.float32,
    )
    real = mixed[:count, :tile] + mixed[count:, tile:]
    imag = mixed[count:, :tile] - mixed[:count, tile:]
    low = lax.broadcasted_iota(jnp.int32, (count, tile), 0)
    high = lax.broadcasted_iota(jnp.int32, (count, tile), 1)
    frequency = low + count * high
    distance = jnp.minimum(frequency, columns - frequency)
    keep = jnp.where(distance < cut, 1.0 / columns, 0.0).astype(jnp.float32)
    mixed = jnp.dot(
        jnp.concatenate([real * keep, imag * keep], axis=0),
        wheel,
        precision=HIGHEST,
        preferred_element_type=jnp.float32,
    )
    real = mixed[:count, :tile] - mixed[count:, tile:]
    imag = mixed[:count, tile:] + mixed[count:, :tile]
    pieces = []
    for t in range(count):
        term = real * turn_cos[t] - imag * turn_sin[t]
        pieces.append(jnp.sum(term, axis=0, keepdims=True))
    return jnp.concatenate(pieces, axis=1)


def split_in_two(values):
    coarse = values.astype(jnp.bfloat16)
    fine = (values - coarse.astype(jnp.float32)).astype(jnp.bfloat16)
    return coarse, fine


def shifted_sum(values, taps, offsets):
    rows = values.shape[0]
    place = lax.broadcasted_iota(jnp.int32, values.shape, 0)
    total = None
    for tap, offset in zip(taps, offsets):
        if offset == 0:
            moved = values
        else:
            moved = pltpu.roll(values, (-offset) % rows, 0)
            if offset > 0:
                moved = jnp.where(place < rows - offset, moved, 0.0)
            else:
                moved = jnp.where(place >= -offset, moved, 0.0)
        term = tap * moved
        total = term if total is None else total + term
    return total


def wave_kernel(
    sizes,
    owner_hbm,
    row_hbm,
    weight_hbm,
    cutoff_hbm,
    profile_hbm,
    wheel_hbm,
    cos_hbm,
    sin_hbm,
    spectra_ref,
    response_ref,
    observed_ref,
    out_ref,
    owner_ref,
    row_ref,
    weight_ref,
    cutoff_ref,
    profile_ref,
    wheel_ref,
    cos_ref,
    sin_ref,
    inbox,
    target,
    table,
    flipped,
    ahead,
    behind,
    data,
    outbox,
    restored,
    resp,
    send_in,
    recv_in,
    send_obs,
    recv_obs,
    send_out,
    recv_out,
    resp_sem,
    small_sem,
    known,
):
    wide, narrow, halves, stokes, rows, tile, count, taps, params = sizes
    half = (taps - 1) // 2
    columns = count * tile
    every = wide * narrow
    my_wide = lax.axis_index("wide")
    my_narrow = lax.axis_index("narrow")
    me = my_wide * narrow + my_narrow

    def wrapped(value, limit):
        return jnp.where(value >= limit, value - limit, value)

    def peer_at(step):
        return wrapped(me + 1 + (step + every // 4 - 1) % (every - 1), every)

    def each(visit):
        for step in range(every - 1):
            visit(step)

    group = 2 if wide % 2 == 0 else 1
    planes = wide // group
    my_plane = lax.div(my_wide, group)
    my_seat = lax.rem(my_wide, group)
    crowd = group * narrow

    def plane_members(offset):
        for dg in range(group):
            for dn in range(narrow):
                if offset or dg or dn:
                    seat = wrapped(my_seat + dg, group)
                    yield (my_plane + offset) * group + seat, wrapped(my_narrow + dn, narrow)

    def members_of(plane, own):
        if own:
            return list(plane_members(0))
        return [
            (plane * group + wrapped(my_seat + dg, group), wrapped(my_narrow + dn, narrow))
            for dg in range(group)
            for dn in range(narrow)
        ]

    across = lax.rem(my_plane + planes // 2, planes)
    if planes == 4:
        far_first = [across, planes - 1 - my_plane, planes - 1 - across, my_plane]
    else:
        far_first = [lax.rem(my_plane + 1 + i, planes) for i in range(planes)]

    def beside(distance, visit):
        @pl.when(my_plane + distance < planes)
        def _():
            visit(distance)

        @pl.when(my_plane >= distance)
        def _():
            visit(-distance)

    def both(peer):
        return (lax.div(peer, narrow), lax.rem(peer, narrow))

    small = [
        pltpu.make_async_copy(source, place, small_sem.at[i])
        for i, (source, place) in enumerate(
            (
                (profile_hbm, profile_ref),
                (cos_hbm, cos_ref),
                (sin_hbm, sin_ref),
                (wheel_hbm, wheel_ref),
                (cutoff_hbm, cutoff_ref),
                (owner_hbm, owner_ref),
                (row_hbm, row_ref),
                (weight_hbm, weight_ref),
            )
        )
    ]
    for copy in small:
        copy.start()
    barrier = pltpu.get_barrier_semaphore()

    def greet(offset):
        for place in plane_members(offset):
            pl.semaphore_signal(barrier, inc=1, device_id=place, device_id_type=MESH)

    greet(0)
    beside(1, greet)
    get_resp = pltpu.make_async_copy(response_ref, resp, resp_sem)
    get_resp.start()
    part = stokes // halves
    mine = []
    for h in range(halves):
        mine.append(
            pltpu.make_async_copy(
                spectra_ref.at[pl.ds(me * stokes + h * part, part)],
                inbox.at[h, my_wide, my_narrow],
                recv_in.at[h, me],
            )
        )
        mine[h].start()
    my_obs = []
    for h in range(halves):
        my_obs.append(
            pltpu.make_async_copy(
                observed_ref.at[pl.ds(my_narrow * stokes + h * part, part)],
                target.at[h, my_narrow],
                recv_obs.at[h, my_narrow],
            )
        )
        my_obs[h].start()

    def spectra_copy(h, peer, place, slot, recv):
        return pltpu.make_async_remote_copy(
            src_ref=spectra_ref.at[pl.ds(peer * stokes + h * part, part)],
            dst_ref=inbox.at[h, slot[0], slot[1]],
            send_sem=send_in.at[h, peer],
            recv_sem=recv_in.at[h, recv],
            device_id=place,
            device_id_type=MESH,
        )

    def observed_copy(h, peer, slot):
        return pltpu.make_async_remote_copy(
            src_ref=observed_ref.at[pl.ds(peer * stokes + h * part, part)],
            dst_ref=target.at[h, slot],
            send_sem=send_obs.at[h, peer],
            recv_sem=recv_obs.at[h, slot],
            device_id=(my_wide, peer),
            device_id_type=MESH,
        )

    def send_first(offset):
        for place in plane_members(offset):
            peer = place[0] * narrow + place[1]
            spectra_copy(0, peer, place, (my_wide, my_narrow), me).start()

    near = jnp.int32(crowd - 1)
    near = near + jnp.where(my_plane + 1 < planes, crowd, 0)
    near = near + jnp.where(my_plane >= 1, crowd, 0)
    pl.semaphore_wait(barrier, near)
    for k in range(1, planes - 1):

        @pl.when((my_plane >= 1) & (my_plane + k < planes))
        def _():
            pl.semaphore_signal(
                known.at[0, k - 1],
                inc=1,
                device_id=(my_wide - group, my_narrow),
                device_id_type=MESH,
            )

        @pl.when((my_plane + 1 < planes) & (my_plane >= k))
        def _():
            pl.semaphore_signal(
                known.at[1, k - 1],
                inc=1,
                device_id=(my_wide + group, my_narrow),
                device_id_type=MESH,
            )

        if k == 1:
            beside(1, send_first)
            send_first(0)
            for step in range(1, narrow):
                observed_copy(0, wrapped(my_narrow + step, narrow), my_narrow).start()

        @pl.when(my_plane + k + 1 < planes)
        def _():
            pl.semaphore_wait(known.at[0, k - 1], 1)

        @pl.when(my_plane >= k + 1)
        def _():
            pl.semaphore_wait(known.at[1, k - 1], 1)

        beside(k + 1, send_first)

    for h in range(1, halves):

        def send_later(step):
            peer = peer_at(step)
            spectra_copy(h, peer, both(peer), (my_wide, my_narrow), me).start()

        each(send_later)
        for step in range(1, narrow):
            observed_copy(h, wrapped(my_narrow + step, narrow), my_narrow).start()

    for copy in small:
        copy.wait()
    kernel_row = band_kernel(
        profile_ref[pl.ds(my_narrow, 1), :],
        cutoff_ref[my_narrow],
        wheel_ref[...],
        cos_ref,
        sin_ref,
        count,
        tile,
    )

    rolled = pltpu.roll(
        jnp.broadcast_to(kernel_row, (tile, columns)), 0, 1, stride=1, stride_axis=0
    )
    for d in range(count):
        block = rolled[:, d * tile : (d + 1) * tile]
        coarse, fine = split_in_two(block)
        table[0, d] = coarse
        table[1, d] = fine
        coarse, fine = split_in_two(block.T)
        flipped[0, d] = coarse
        flipped[1, d] = fine

    for s in range(count):
        plane, seat = divmod(s, group)
        inner = slice(seat * tile, (seat + 1) * tile)
        place = jnp.int32(0)
        for t in range(count):
            place = jnp.where(owner_ref[t] == s, t, place)
        for b in range(count):
            up = lax.rem(b - place + count, count)
            down = lax.rem(b + count - place, count)
            for fine in range(2):
                ahead[fine, plane, inner, b * tile : (b + 1) * tile] = table[fine, up]
                behind[fine, plane, b * tile : (b + 1) * tile, inner] = flipped[fine, down]

    tap_values = [row_ref[my_narrow, k] for k in range(taps)]
    strips = narrow * rows

    def back_copy(h, peer, recv):
        to_wide, to_narrow = both(peer)
        return pltpu.make_async_remote_copy(
            src_ref=outbox.at[h, to_wide, to_narrow],
            dst_ref=restored.at[h, recv],
            send_sem=send_out.at[h, peer],
            recv_sem=recv_out.at[h, recv],
            device_id=(to_wide, to_narrow),
            device_id_type=MESH,
        )

    for h in range(halves):
        mine[h].wait()
        image = None
        for i, plane in enumerate(reversed(far_first)):
            for place in members_of(plane, i == 0):
                peer = place[0] * narrow + place[1]
                spectra_copy(h, peer, place, place, peer).wait_recv()
            ordered = []
            for dg in range(group):
                got = inbox[h, plane * group + dg].astype(jnp.float32)
                ordered.append(
                    jnp.concatenate(
                        [got[n, c] for c in range(part) for n in range(narrow)], axis=0
                    )
                )
            ordered = jnp.concatenate(ordered, axis=1).astype(jnp.bfloat16)
            for fine in range(2):
                term = jnp.dot(ordered, ahead[fine, plane], preferred_element_type=jnp.float32)
                image = term if image is None else image + term
        image = image.astype(jnp.bfloat16).astype(jnp.float32)

        my_obs[h].wait()
        for step in range(1, narrow):
            peer = wrapped(my_narrow + step, narrow)
            observed_copy(h, peer, peer).wait_recv()

        for c in range(part):
            lines = image[c * strips : (c + 1) * strips]
            blurred = shifted_sum(lines, tap_values, [k - half for k in range(taps)])
            seen = jnp.concatenate(
                [target[h, n, c].astype(jnp.float32) for n in range(narrow)], axis=0
            )
            misfit = weight_ref[my_narrow * stokes + h * part + c] * (blurred - seen)
            misfit = misfit.astype(jnp.bfloat16).astype(jnp.float32)
            spread = shifted_sum(misfit, tap_values, [half - k for k in range(taps)])
            data[c * strips : (c + 1) * strips, :] = spread.astype(jnp.bfloat16)

        values = data[...]
        for i, plane in enumerate(far_first):
            back = jnp.dot(
                values, behind[0, plane], preferred_element_type=jnp.float32
            ) + jnp.dot(values, behind[1, plane], preferred_element_type=jnp.float32)
            for dg in range(group):
                for n in range(narrow):
                    for c in range(part):
                        top = (c * narrow + n) * rows
                        outbox[h, plane * group + dg, n, c] = back[
                            top : top + rows, dg * tile : (dg + 1) * tile
                        ].astype(jnp.bfloat16)
            for place in members_of(plane, i == planes - 1):
                back_copy(h, place[0] * narrow + place[1], me).start()

    get_resp.wait()

    def project(h, wave, block, totals):
        for c in range(part):
            pixel = block[c].astype(jnp.float32)
            totals = [
                total + resp[p, wave * stokes + h * part + c].astype(jnp.float32) * pixel
                for p, total in enumerate(totals)
            ]
        return totals

    totals = [jnp.zeros((rows, tile), jnp.float32) for _ in range(params)]
    for h in range(halves):
        totals = project(h, me, outbox[h, my_wide, my_narrow], totals)

        def take_back(step, totals):
            peer = lax.rem(me + 1 + step, every)
            back_copy(h, peer, peer).wait_recv()
            return project(h, peer, restored[h, peer], totals)

        totals = lax.fori_loop(0, every - 1, take_back, totals)
    for p in range(params):
        out_ref[p] = totals[p]

    for h in range(halves):

        def finish(step):
            peer = peer_at(step)
            spectra_copy(h, peer, both(peer), (my_wide, my_narrow), me).wait_send()
            back_copy(h, peer, me).wait_send()

        each(finish)
        for step in range(1, narrow):
            observed_copy(h, wrapped(my_narrow + step, narrow), my_narrow).wait_send()


def wave_plan(
    spectra, response, observed, column_profile, row_kernel, noise_weight, cutoff, owner
):
    channels, rows, tile = spectra.shape
    params = response.shape[0]
    waves, columns = column_profile.shape
    count = owner.shape[0]
    wide = lax.axis_size("wide")
    narrow = lax.axis_size("narrow")
    every = wide * narrow
    stokes = channels // every
    taps = row_kernel.shape[1]
    group = 2 if wide % 2 == 0 else 1
    halves = HALVES if stokes % HALVES == 0 else 1
    part = stokes // halves
    sizes = (wide, narrow, halves, stokes, rows, tile, count, taps, params)
    vmem = pl.BlockSpec(memory_space=pltpu.VMEM)
    hbm = pl.BlockSpec(memory_space=pltpu.HBM)
    dma = pltpu.SemaphoreType.DMA
    half_type = jnp.bfloat16
    lines = part * narrow * rows
    tables = phase_constants(count, tile)
    return pl.pallas_call(
        functools.partial(wave_kernel, sizes),
        out_shape=jax.ShapeDtypeStruct((params, rows, tile), jnp.float32),
        in_specs=[hbm] * 11,
        out_specs=vmem,
        scratch_shapes=[
            pltpu.SMEM(owner.shape, jnp.int32),
            pltpu.SMEM(row_kernel.shape, jnp.float32),
            pltpu.SMEM(noise_weight.shape, jnp.float32),
            pltpu.SMEM(cutoff.shape, jnp.int32),
            pltpu.VMEM(column_profile.shape, jnp.float32),
            *[pltpu.VMEM(table.shape, jnp.float32) for table in tables],
            pltpu.VMEM((halves, wide, narrow, part, rows, tile), half_type),
            pltpu.VMEM((halves, narrow, part, rows, columns), half_type),
            pltpu.VMEM((2, count, tile, tile), half_type),
            pltpu.VMEM((2, count, tile, tile), half_type),
            pltpu.VMEM((2, wide // group, group * tile, columns), half_type),
            pltpu.VMEM((2, wide // group, columns, group * tile), half_type),
            pltpu.VMEM((lines, columns), half_type),
            pltpu.VMEM((halves, wide, narrow, part, rows, tile), half_type),
            pltpu.VMEM((halves, every, part, rows, tile), half_type),
            pltpu.VMEM(response.shape, half_type),
            dma((halves, every)),
            dma((halves, every)),
            dma((halves, narrow)),
            dma((halves, narrow)),
            dma((halves, every)),
            dma((halves, every)),
            dma,
            dma((8,)),
            pltpu.SemaphoreType.REGULAR((2, max(wide, 2))),
        ],
        compiler_params=pltpu.CompilerParams(
            collective_id=0, has_side_effects=True, vmem_limit_bytes=60 * 1024 * 1024
        ),
    )(
        owner,
        row_kernel,
        noise_weight,
        cutoff,
        column_profile,
        *tables,
        spectra,
        response,
        observed,
    )


def per_device(
    spectra, response, observed, column_profile, row_kernel, noise_weight, cutoff, owner
):
    channels, rows, tile = spectra.shape
    waves, columns = column_profile.shape
    count = owner.shape[0]
    one_each = waves == lax.axis_size("narrow") and count == lax.axis_size("wide")
    plan = wave_plan if one_each and rows == 8 and tile == 128 else strip_plan
    return plan(
        spectra, response, observed, column_profile, row_kernel, noise_weight, cutoff, owner
    )


def solution(mesh):
    return jax.shard_map(
        per_device,
        mesh=mesh,
        in_specs=(
            P(None, "narrow", "wide"),
            P(None, None, "narrow", "wide"),
            P("wide", "narrow", None),
            P("wide", None),
            P("wide", None),
            P("wide"),
            P("wide"),
            P(),
        ),
        out_specs=P(None, "narrow", "wide"),
        check_vma=False,
    )
```

profile of v0, /device:TPU:0, one launch (start us, length us, event | category | flops | bytes accessed | tf_op | source)
XLA Modules:
  0.0 26.7 jit_solution(5282311584370085022)
XLA Ops:
  0.0 25.2 %shard_map.109 = f32[12,8,128]{2,1,0:T(8,128)} custom-call(s32[8]{0:T(128)} %owner_hbm.1, f32[4,5]{1,0:T(4,128)} %row_hbm.1, f32[16]{0:T(128)} %weight_hbm.1, s32[4]{0:T(128)} %cutoff_hbm.1, f32[4,1024]{1,0:T(4,128)} %profile_hbm.1, f32[128,256]{1,0:T(8,128)} %constant.6.clone.wheel_hbm, f32[8,8,128]{2,1,0:T(8,128)} %constant.7.clone.cos_hbm, ...), custom_call_target="tpu_custom_call" | custom-call | tf_op jit(solution)/shard_map/pallas_call | solution.py:626
  25.2 1.4 %copy.13 = f32[12,8,128]{2,1,0:T(8,128)} copy(f32[12,8,128]{2,1,0:T(8,128)} %shard_map.109) | data formatting | bytes 98304
where the time goes:
time: 26.8 us; the launch traced here: 26.7 us
  Pallas kernels  25.2 us (94%)
  local copies, waits for them, and re-layouts  1.42 us (5%)
    pallas_call x1, Pallas kernels, wave_plan(): pl.pallas_call(functools.partial(wave_kernel, sizes), out_shape=jax.Shape...  25.2 us
    unnamed x1, local copies, waits for them, and re-layouts  1.42 us

commit v1 on v0

--- a/solution.py
+++ b/solution.py
@@ -291,52 +291,37 @@
     def wrapped(value, limit):
         return jnp.where(value >= limit, value - limit, value)
 
-    def peer_at(step):
-        return wrapped(me + 1 + (step + every // 4 - 1) % (every - 1), every)
-
-    def each(visit):
-        for step in range(every - 1):
-            visit(step)
-
     group = 2 if wide % 2 == 0 else 1
+    pair = 2 if narrow % 2 == 0 else 1
     planes = wide // group
+    crowd = group * narrow
+    part = stokes // halves
     my_plane = lax.div(my_wide, group)
     my_seat = lax.rem(my_wide, group)
-    crowd = group * narrow
-
-    def plane_members(offset):
+    my_chip = lax.div(my_narrow, pair)
+    my_core = lax.rem(my_narrow, pair)
+    chips = narrow // pair
+
+    def members_of(plane, own):
+        found = []
         for dg in range(group):
-            for dn in range(narrow):
-                if offset or dg or dn:
+            for dx in range(chips):
+                for dc in range(pair):
+                    if own and dg == 0 and dx == 0 and dc == 0:
+                        continue
                     seat = wrapped(my_seat + dg, group)
-                    yield (my_plane + offset) * group + seat, wrapped(my_narrow + dn, narrow)
-
-    def members_of(plane, own):
-        if own:
-            return list(plane_members(0))
-        return [
-            (plane * group + wrapped(my_seat + dg, group), wrapped(my_narrow + dn, narrow))
-            for dg in range(group)
-            for dn in range(narrow)
-        ]
+                    chip = wrapped(my_chip + dx, chips)
+                    core = wrapped(my_core + dc, pair)
+                    found.append((plane * group + seat, chip * pair + core))
+        return found
 
     across = lax.rem(my_plane + planes // 2, planes)
     if planes == 4:
         far_first = [across, planes - 1 - my_plane, planes - 1 - across, my_plane]
     else:
         far_first = [lax.rem(my_plane + 1 + i, planes) for i in range(planes)]
-
-    def beside(distance, visit):
-        @pl.when(my_plane + distance < planes)
-        def _():
-            visit(distance)
-
-        @pl.when(my_plane >= distance)
-        def _():
-            visit(-distance)
-
-    def both(peer):
-        return (lax.div(peer, narrow), lax.rem(peer, narrow))
+    others = far_first[:-1]
+    line = pair
 
     small = [
         pltpu.make_async_copy(source, place, small_sem.at[i])
@@ -353,114 +338,71 @@
             )
         )
     ]
+    barrier = pltpu.get_barrier_semaphore()
+    neighbours = members_of(my_plane, True)
+    for plane in others:
+        neighbours = neighbours + members_of(plane, False)[:line]
+    for place in neighbours:
+        pl.semaphore_signal(barrier, inc=1, device_id=place, device_id_type=MESH)
     for copy in small:
         copy.start()
-    barrier = pltpu.get_barrier_semaphore()
-
-    def greet(offset):
-        for place in plane_members(offset):
-            pl.semaphore_signal(barrier, inc=1, device_id=place, device_id_type=MESH)
-
-    greet(0)
-    beside(1, greet)
+    for h in range(halves):
+        pltpu.make_async_copy(
+            spectra_ref.at[pl.ds(me * stokes + h * part, part)],
+            inbox.at[h, my_wide, my_narrow],
+            recv_in.at[h, my_plane],
+        ).start()
+        pltpu.make_async_copy(
+            observed_ref.at[pl.ds(my_narrow * stokes + h * part, part)],
+            target.at[h, my_narrow],
+            recv_obs.at[h],
+        ).start()
     get_resp = pltpu.make_async_copy(response_ref, resp, resp_sem)
     get_resp.start()
-    part = stokes // halves
-    mine = []
-    for h in range(halves):
-        mine.append(
-            pltpu.make_async_copy(
-                spectra_ref.at[pl.ds(me * stokes + h * part, part)],
-                inbox.at[h, my_wide, my_narrow],
-                recv_in.at[h, me],
-            )
-        )
-        mine[h].start()
-    my_obs = []
-    for h in range(halves):
-        my_obs.append(
-            pltpu.make_async_copy(
-                observed_ref.at[pl.ds(my_narrow * stokes + h * part, part)],
-                target.at[h, my_narrow],
-                recv_obs.at[h, my_narrow],
-            )
-        )
-        my_obs[h].start()
-
-    def spectra_copy(h, peer, place, slot, recv):
-        return pltpu.make_async_remote_copy(
+
+    def send_spectra(h, place):
+        peer = place[0] * narrow + place[1]
+        pltpu.make_async_remote_copy(
             src_ref=spectra_ref.at[pl.ds(peer * stokes + h * part, part)],
-            dst_ref=inbox.at[h, slot[0], slot[1]],
-            send_sem=send_in.at[h, peer],
-            recv_sem=recv_in.at[h, recv],
+            dst_ref=inbox.at[h, my_wide, my_narrow],
+            send_sem=send_in,
+            recv_sem=recv_in.at[h, my_plane],
             device_id=place,
             device_id_type=MESH,
-        )
-
-    def observed_copy(h, peer, slot):
-        return pltpu.make_async_remote_copy(
-            src_ref=observed_ref.at[pl.ds(peer * stokes + h * part, part)],
-            dst_ref=target.at[h, slot],
-            send_sem=send_obs.at[h, peer],
-            recv_sem=recv_obs.at[h, slot],
-            device_id=(my_wide, peer),
-            device_id_type=MESH,
-        )
-
-    def send_first(offset):
-        for place in plane_members(offset):
-            peer = place[0] * narrow + place[1]
-            spectra_copy(0, peer, place, (my_wide, my_narrow), me).start()
-
-    near = jnp.int32(crowd - 1)
-    near = near + jnp.where(my_plane + 1 < planes, crowd, 0)
-    near = near + jnp.where(my_plane >= 1, crowd, 0)
-    pl.semaphore_wait(barrier, near)
-    for k in range(1, planes - 1):
-
-        @pl.when((my_plane >= 1) & (my_plane + k < planes))
-        def _():
-            pl.semaphore_signal(
-                known.at[0, k - 1],
-                inc=1,
-                device_id=(my_wide - group, my_narrow),
+        ).start()
+
+    def send_observed(h):
+        for step in range(1, narrow):
+            peer = wrapped(my_narrow + step, narrow)
+            pltpu.make_async_remote_copy(
+                src_ref=observed_ref.at[pl.ds(peer * stokes + h * part, part)],
+                dst_ref=target.at[h, my_narrow],
+                send_sem=send_obs,
+                recv_sem=recv_obs.at[h],
+                device_id=(my_wide, peer),
                 device_id_type=MESH,
-            )
-
-        @pl.when((my_plane + 1 < planes) & (my_plane >= k))
-        def _():
-            pl.semaphore_signal(
-                known.at[1, k - 1],
-                inc=1,
-                device_id=(my_wide + group, my_narrow),
-                device_id_type=MESH,
-            )
-
-        if k == 1:
-            beside(1, send_first)
-            send_first(0)
-            for step in range(1, narrow):
-                observed_copy(0, wrapped(my_narrow + step, narrow), my_narrow).start()
-
-        @pl.when(my_plane + k + 1 < planes)
-        def _():
-            pl.semaphore_wait(known.at[0, k - 1], 1)
-
-        @pl.when(my_plane >= k + 1)
-        def _():
-            pl.semaphore_wait(known.at[1, k - 1], 1)
-
-        beside(k + 1, send_first)
-
+            ).start()
+
+    pl.semaphore_wait(barrier, len(neighbours))
+    for place in members_of(my_plane, True):
+        pl.semaphore_signal(known, inc=1, device_id=place, device_id_type=MESH)
+    for plane in others:
+        for place in members_of(plane, False)[:line]:
+            send_spectra(0, place)
+    for place in members_of(my_plane, True):
+        send_spectra(0, place)
+    pl.semaphore_wait(known, crowd - 1)
+    for plane in others:
+        for place in members_of(plane, False)[line:]:
+            send_spectra(0, place)
+    send_observed(0)
     for h in range(1, halves):
-
-        def send_later(step):
-            peer = peer_at(step)
-            spectra_copy(h, peer, both(peer), (my_wide, my_narrow), me).start()
-
-        each(send_later)
-        for step in range(1, narrow):
-            observed_copy(h, wrapped(my_narrow + step, narrow), my_narrow).start()
+        for plane in others:
+            for place in members_of(plane, False):
+                send_spectra(h, place)
+        for place in members_of(my_plane, True):
+            send_spectra(h, place)
+        send_observed(h)
 
     for copy in small:
         copy.wait()
@@ -502,24 +444,11 @@
     tap_values = [row_ref[my_narrow, k] for k in range(taps)]
     strips = narrow * rows
 
-    def back_copy(h, peer, recv):
-        to_wide, to_narrow = both(peer)
-        return pltpu.make_async_remote_copy(
-            src_ref=outbox.at[h, to_wide, to_narrow],
-            dst_ref=restored.at[h, recv],
-            send_sem=send_out.at[h, peer],
-            recv_sem=recv_out.at[h, recv],
-            device_id=(to_wide, to_narrow),
-            device_id_type=MESH,
-        )
-
     for h in range(halves):
-        mine[h].wait()
         image = None
-        for i, plane in enumerate(reversed(far_first)):
-            for place in members_of(plane, i == 0):
-                peer = place[0] * narrow + place[1]
-                spectra_copy(h, peer, place, place, peer).wait_recv()
+        for plane in reversed(far_first):
+            box = inbox.at[h, pl.ds(plane * group, group)]
+            pltpu.make_async_copy(box, box, recv_in.at[h, plane]).wait()
             ordered = []
             for dg in range(group):
                 got = inbox[h, plane * group + dg].astype(jnp.float32)
@@ -534,10 +463,7 @@
                 image = term if image is None else image + term
         image = image.astype(jnp.bfloat16).astype(jnp.float32)
 
-        my_obs[h].wait()
-        for step in range(1, narrow):
-            peer = wrapped(my_narrow + step, narrow)
-            observed_copy(h, peer, peer).wait_recv()
+        pltpu.make_async_copy(target.at[h], target.at[h], recv_obs.at[h]).wait()
 
         for c in range(part):
             lines = image[c * strips : (c + 1) * strips]
@@ -563,42 +489,46 @@
                             top : top + rows, dg * tile : (dg + 1) * tile
                         ].astype(jnp.bfloat16)
             for place in members_of(plane, i == planes - 1):
-                back_copy(h, place[0] * narrow + place[1], me).start()
+                pltpu.make_async_remote_copy(
+                    src_ref=outbox.at[h, place[0], place[1]],
+                    dst_ref=restored.at[h, me],
+                    send_sem=send_out.at[h],
+                    recv_sem=recv_out.at[h, my_plane],
+                    device_id=place,
+                    device_id_type=MESH,
+                ).start()
+        pltpu.make_async_copy(
+            outbox.at[h, my_wide, my_narrow], restored.at[h, me], recv_out.at[h, my_plane]
+        ).start()
 
     get_resp.wait()
-
-    def project(h, wave, block, totals):
-        for c in range(part):
-            pixel = block[c].astype(jnp.float32)
-            totals = [
-                total + resp[p, wave * stokes + h * part + c].astype(jnp.float32) * pixel
-                for p, total in enumerate(totals)
-            ]
-        return totals
-
     totals = [jnp.zeros((rows, tile), jnp.float32) for _ in range(params)]
     for h in range(halves):
-        totals = project(h, me, outbox[h, my_wide, my_narrow], totals)
-
-        def take_back(step, totals):
-            peer = lax.rem(me + 1 + step, every)
-            back_copy(h, peer, peer).wait_recv()
-            return project(h, peer, restored[h, peer], totals)
-
-        totals = lax.fori_loop(0, every - 1, take_back, totals)
+        for plane in reversed(far_first):
+            box = restored.at[h, pl.ds(plane * crowd, crowd)]
+            pltpu.make_async_copy(box, box, recv_out.at[h, plane]).wait()
+
+            def project(step, totals):
+                peer = plane * crowd + step
+                for c in range(part):
+                    pixel = restored[h, peer, c].astype(jnp.float32)
+                    totals = [
+                        total + resp[p, peer * stokes + h * part + c].astype(jnp.float32) * pixel
+                        for p, total in enumerate(totals)
+                    ]
+                return totals
+
+            totals = lax.fori_loop(0, crowd, project, totals)
     for p in range(params):
         out_ref[p] = totals[p]
 
+    sent = spectra_ref.at[pl.ds(0, (every - 1) * stokes)]
+    pltpu.make_async_copy(sent, sent, send_in).wait()
+    sent = observed_ref.at[pl.ds(0, (narrow - 1) * stokes)]
+    pltpu.make_async_copy(sent, sent, send_obs).wait()
     for h in range(halves):
-
-        def finish(step):
-            peer = peer_at(step)
-            spectra_copy(h, peer, both(peer), (my_wide, my_narrow), me).wait_send()
-            back_copy(h, peer, me).wait_send()
-
-        each(finish)
-        for step in range(1, narrow):
-            observed_copy(h, wrapped(my_narrow + step, narrow), my_narrow).wait_send()
+        sent = restored.at[h, pl.ds(0, every - 1)]
+        pltpu.make_async_copy(sent, sent, send_out.at[h]).wait()
 
 
 def wave_plan(
@@ -625,7 +555,7 @@
     tables = phase_constants(count, tile)
     return pl.pallas_call(
         functools.partial(wave_kernel, sizes),
-        out_shape=jax.ShapeDtypeStruct((params, rows, tile), jnp.float32),
+        out_shape=pltpu.VMEM((params, rows, tile), jnp.float32),
         in_specs=[hbm] * 11,
         out_specs=vmem,
         scratch_shapes=[
@@ -645,15 +575,15 @@
             pltpu.VMEM((halves, wide, narrow, part, rows, tile), half_type),
             pltpu.VMEM((halves, every, part, rows, tile), half_type),
             pltpu.VMEM(response.shape, half_type),
-            dma((halves, every)),
-            dma((halves, every)),
-            dma((halves, narrow)),
-            dma((halves, narrow)),
-            dma((halves, every)),
-            dma((halves, every)),
+            dma,
+            dma((halves, wide // group)),
+            dma,
+            dma((halves,)),
+            dma((halves,)),
+            dma((halves, wide // group)),
             dma,
             dma((8,)),
-            pltpu.SemaphoreType.REGULAR((2, max(wide, 2))),
+            pltpu.SemaphoreType.REGULAR,
         ],
         compiler_params=pltpu.CompilerParams(
             collective_id=0, has_side_effects=True, vmem_limit_bytes=60 * 1024 * 1024

time: 26.8 us -> 24.6 us (0.918)
  Pallas kernels: 25.2 us -> 23.8 us
  local copies, waits for them, and re-layouts: 1.42 us -> 0.62 us
    pallas_call x1, Pallas kernels: 25.2 us -> 23.8 us  [wave_plan(): pl.pallas_call(functools.partial(wave_kernel, sizes), out_shape=pltpu.VME...]
    unnamed x1, local copies, waits for them, and re-layouts: 1.42 us -> 0.62 us
where the time goes in v1:
time: 24.6 us; the launch traced here: 24.5 us
  Pallas kernels  23.8 us (97%)
  local copies, waits for them, and re-layouts  0.62 us (3%)
    pallas_call x1, Pallas kernels, wave_plan(): pl.pallas_call(functools.partial(wave_kernel, sizes), out_shape=pltpu.VME...  23.8 us
    unnamed x1, local copies, waits for them, and re-layouts  0.62 us

profile of v1, /device:TPU:0, one launch (start us, length us, event | category | flops | bytes accessed | tf_op | source)
XLA Modules:
  0.0 24.5 jit_solution(12595302558230819248)
XLA Ops:
  0.0 23.8 %shard_map.109 = f32[12,8,128]{2,1,0:T(8,128)S(1)} custom-call(s32[8]{0:T(128)} %owner_hbm.1, f32[4,5]{1,0:T(4,128)} %row_hbm.1, f32[16]{0:T(128)} %weight_hbm.1, s32[4]{0:T(128)} %cutoff_hbm.1, f32[4,1024]{1,0:T(4,128)} %profile_hbm.1, f32[128,256]{1,0:T(8,128)} %constant.6.clone.wheel_hbm, f32[8,8,128]{2,1,0:T(8,128)} %constant.7.clone.cos_hbm, ...), custom_call_target="tpu_custom_call" | custom-call | tf_op jit(solution)/shard_map/pallas_call | solution.py:556
  23.9 0.6 %copy.13 = f32[12,8,128]{2,1,0:T(8,128)} copy(f32[12,8,128]{2,1,0:T(8,128)S(1)} %shard_map.109) | data formatting | bytes 98304

commit v2 on v1

--- a/solution.py
+++ b/solution.py
@@ -159,7 +159,7 @@
     return jnp.einsum("pcrx,crx->prx", response, pixels, preferred_element_type=jnp.float32)
 
 
-HALVES = 1
+HALVES = 2
 MESH = pl.DeviceIdType.MESH
 HIGHEST = lax.Precision.HIGHEST
 
@@ -279,6 +279,8 @@
     resp_sem,
     small_sem,
     known,
+    stage,
+    stage_sem,
 ):
     wide, narrow, halves, stokes, rows, tile, count, taps, params = sizes
     half = (taps - 1) // 2
@@ -321,6 +323,16 @@
     else:
         far_first = [lax.rem(my_plane + 1 + i, planes) for i in range(planes)]
     others = far_first[:-1]
+    if planes == 4:
+        odd = lax.rem(my_plane, 2) == 1
+        back_first = [
+            jnp.where(odd, 0, across),
+            jnp.where(odd, planes - my_plane, planes - 1 - my_plane),
+            jnp.where(odd, 2, planes - 1 - across),
+            my_plane,
+        ]
+    else:
+        back_first = far_first
     line = pair
 
     small = [
@@ -357,13 +369,15 @@
             target.at[h, my_narrow],
             recv_obs.at[h],
         ).start()
+    get_stage = pltpu.make_async_copy(spectra_ref, stage, stage_sem)
+    get_stage.start()
     get_resp = pltpu.make_async_copy(response_ref, resp, resp_sem)
     get_resp.start()
 
     def send_spectra(h, place):
         peer = place[0] * narrow + place[1]
         pltpu.make_async_remote_copy(
-            src_ref=spectra_ref.at[pl.ds(peer * stokes + h * part, part)],
+            src_ref=stage.at[pl.ds(peer * stokes + h * part, part)],
             dst_ref=inbox.at[h, my_wide, my_narrow],
             send_sem=send_in,
             recv_sem=recv_in.at[h, my_plane],
@@ -383,6 +397,7 @@
                 device_id_type=MESH,
             ).start()
 
+    get_stage.wait()
     pl.semaphore_wait(barrier, len(neighbours))
     for place in members_of(my_plane, True):
         pl.semaphore_signal(known, inc=1, device_id=place, device_id_type=MESH)
@@ -477,7 +492,7 @@
             data[c * strips : (c + 1) * strips, :] = spread.astype(jnp.bfloat16)
 
         values = data[...]
-        for i, plane in enumerate(far_first):
+        for i, plane in enumerate(back_first):
             back = jnp.dot(
                 values, behind[0, plane], preferred_element_type=jnp.float32
             ) + jnp.dot(values, behind[1, plane], preferred_element_type=jnp.float32)
@@ -488,7 +503,13 @@
                         outbox[h, plane * group + dg, n, c] = back[
                             top : top + rows, dg * tile : (dg + 1) * tile
                         ].astype(jnp.bfloat16)
-            for place in members_of(plane, i == planes - 1):
+            if i < planes - 1:
+                places = [
+                    (plane * group + seat, n) for seat in range(group) for n in range(narrow)
+                ]
+            else:
+                places = members_of(plane, True)
+            for place in places:
                 pltpu.make_async_remote_copy(
                     src_ref=outbox.at[h, place[0], place[1]],
                     dst_ref=restored.at[h, me],
@@ -584,6 +605,8 @@
             dma,
             dma((8,)),
             pltpu.SemaphoreType.REGULAR,
+            pltpu.VMEM(spectra.shape, half_type),
+            dma,
         ],
         compiler_params=pltpu.CompilerParams(
             collective_id=0, has_side_effects=True, vmem_limit_bytes=60 * 1024 * 1024

time: 24.6 us -> 22.9 us (0.931)
  Pallas kernels: 23.8 us -> 22.1 us
    pallas_call x1, Pallas kernels: 23.8 us -> 22.1 us  [wave_plan(): pl.pallas_call(functools.partial(wave_kernel, sizes), out_shape=pltpu.VME...]
where the time goes in v2:
time: 22.9 us; the launch traced here: 22.8 us
  Pallas kernels  22.1 us (97%)
  local copies, waits for them, and re-layouts  0.62 us (3%)
    pallas_call x1, Pallas kernels, wave_plan(): pl.pallas_call(functools.partial(wave_kernel, sizes), out_shape=pltpu.VME...  22.1 us
    unnamed x1, local copies, waits for them, and re-layouts  0.62 us

profile of v2, /device:TPU:0, one launch (start us, length us, event | category | flops | bytes accessed | tf_op | source)
XLA Modules:
  0.0 22.8 jit_solution(15981486732013369077)
XLA Ops:
  0.0 22.1 %shard_map.109 = f32[12,8,128]{2,1,0:T(8,128)S(1)} custom-call(s32[8]{0:T(128)} %owner_hbm.1, f32[4,5]{1,0:T(4,128)} %row_hbm.1, f32[16]{0:T(128)} %weight_hbm.1, s32[4]{0:T(128)} %cutoff_hbm.1, f32[4,1024]{1,0:T(4,128)} %profile_hbm.1, f32[128,256]{1,0:T(8,128)} %constant.6.clone.wheel_hbm, f32[8,8,128]{2,1,0:T(8,128)} %constant.7.clone.cos_hbm, ...), custom_call_target="tpu_custom_call" | custom-call | tf_op jit(solution)/shard_map/pallas_call | solution.py:577
  22.1 0.6 %copy.13 = f32[12,8,128]{2,1,0:T(8,128)} copy(f32[12,8,128]{2,1,0:T(8,128)S(1)} %shard_map.109) | data formatting | bytes 98304
